TPU v7x, 32 devices: a whole 2x2x4 slice. The times are simulated.
32 devices in a mesh: rows: 8 (over z, y), cols: 4 (over x, core).
Axes of the slice: x: 2, y: 2, z: 4, core: 2. Of those that a mesh axis runs over, the one named last changes fastest.
Arguments:
- feats_t: bfloat16 [128, 16384], P('cols', 'rows'), may hold values from -6 to 6
- adj_index: int32 [128, 16], replicated, may hold values from 0 to 127, as said below
- adj_weight: bfloat16 [128, 16, 128, 128], P('rows'), as said below
- weight: bfloat16 [128, 256], replicated, may hold values from -0.5 to 0.5
- cotangent_t: bfloat16 [256, 16384], P('cols', 'rows'), may hold values from -6 to 6
Outputs:
- output_t: bfloat16 [256, 16384], P('cols', 'rows')
- weight_grad: float32 [128, 256], P('cols')
- feat_grad: float32 [128, 16384], P('cols', 'rows')
Inputs may be any that keep to these rules, and one draw needn't show every extreme that they name: `adj_index`: slot 0 of row block i names block i itself. Blocks are grouped 16 to a device in order. Slot 1 names a block of the next device (device index plus one, cyclically). The row blocks of one device name at most 4 distinct blocks of any other device, and exactly 4 of the next one. A block may stand in several slots of one row block. `adj_weight`: Nonnegative; about one entry in eight is nonzero.
All inputs are finite; a program needn't handle non-finite values.
Results may differ from a plain program's by a relative error of at most 0.0054.
Values may be sent and summed in bfloat16 or wider, within the bound.
No kernel may reach another device: no remote copies, remote signals or barrier semaphores. Data moves between devices by JAX's collectives and lax.ppermute only.
A program may use at most 128 MiB of HBM per device.

v0:
```python
import math
import jax
import jax.numpy as jnp
from jax import lax
from jax.sharding import PartitionSpec as P

CAP = 4


def body(feats_t, adj_index, adj_weight, weight, cotangent_t):
    feat_rows, node_cols = feats_t.shape
    blocks_n = adj_weight.shape[0]
    slots_n = adj_weight.shape[1]
    tile_n = adj_weight.shape[2]
    row_devs = lax.axis_size("rows")
    row_pos = lax.axis_index("rows")
    col_pos = lax.axis_index("cols")
    unit_rows = cotangent_t.shape[0]
    own_index = lax.dynamic_slice_in_dim(adj_index, row_pos * blocks_n, blocks_n, 0)
    own_flat = own_index.reshape(-1)
    local_tiles = feats_t.reshape(feat_rows, blocks_n, tile_n).transpose(1, 0, 2)
    device_ids = jnp.arange(row_devs, dtype=jnp.int32)
    slot_ids = jnp.arange(CAP, dtype=jnp.int32)
    mine = row_pos * blocks_n + jnp.arange(blocks_n, dtype=jnp.int32)
    peers_index = adj_index.reshape(row_devs, blocks_n * slots_n)
    wanted = (
        jnp.any(peers_index[:, :, None] == mine[None, None, :], axis=1)
        & (device_ids != row_pos)[:, None]
    )
    ordinal = jnp.cumsum(wanted.astype(jnp.int32), axis=1) - 1
    selector = wanted[:, None, :] & (ordinal[:, None, :] == slot_ids[None, :, None])
    source = own_flat // blocks_n
    block_pos = own_flat % blocks_n
    needed = jnp.any(
        own_flat[:, None] == jnp.arange(row_devs * blocks_n, dtype=jnp.int32)[None, :], axis=0
    )
    needed = needed.reshape(row_devs, blocks_n) & (device_ids != row_pos)[:, None]
    need_order = jnp.cumsum(needed.astype(jnp.int32), axis=1) - 1
    slot_of = source * CAP + need_order.reshape(-1)[own_flat]
    remote = source != row_pos
    outgoing = jnp.einsum(
        "pcb,bfj->pcfj",
        selector.astype(jnp.bfloat16),
        local_tiles,
        preferred_element_type=jnp.float32,
    ).astype(jnp.bfloat16)
    incoming = lax.all_to_all(outgoing, "rows", split_axis=0, concat_axis=0, tiled=True)
    received = incoming.reshape(row_devs * CAP, feat_rows, tile_n)[slot_of]
    own_part = local_tiles[block_pos]
    picked = jnp.where(remote[:, None, None], received, own_part).reshape(
        blocks_n, slots_n, feat_rows, tile_n
    )
    aggregate = jnp.einsum("bkfj,bkij->fbi", picked, adj_weight, preferred_element_type=jnp.float32)
    aggregated = aggregate.reshape(feat_rows, node_cols).astype(jnp.bfloat16)
    w_slab = lax.dynamic_slice_in_dim(weight, col_pos * unit_rows, unit_rows, 1)
    pre_act = lax.dot_general(
        w_slab,
        lax.all_gather(aggregated, "cols", axis=0, tiled=True),
        (((0,), (0,)), ((), ())),
        preferred_element_type=jnp.float32,
    )
    output_t = jax.nn.silu(pre_act).astype(jnp.bfloat16)
    sigm = jax.nn.sigmoid(pre_act)
    pre_grad = (cotangent_t.astype(jnp.float32) * sigm * (1.0 + pre_act * (1.0 - sigm))).astype(
        jnp.bfloat16
    )
    w_mine = lax.dynamic_slice_in_dim(weight, col_pos * feat_rows, feat_rows, 0)
    portion = lax.all_gather(pre_grad, "cols", axis=0, tiled=True)
    grad_acc = jnp.dot(w_mine, portion, preferred_element_type=jnp.float32)
    block_grad = lax.dot_general(
        aggregated, portion, (((1,), (1,)), ((), ())), preferred_element_type=jnp.float32
    )
    grad_scale = 1.0 / math.sqrt(node_cols * row_devs)
    weight_grad = lax.psum(block_grad, "rows") * grad_scale
    agg_grad = grad_acc.astype(jnp.bfloat16)
    contrib = jnp.einsum(
        "fbi,bkij->bkfj",
        agg_grad.reshape(feat_rows, blocks_n, tile_n),
        adj_weight,
        preferred_element_type=jnp.float32,
    )
    contrib_flat = contrib.reshape(blocks_n * slots_n, feat_rows * tile_n)
    slot_total = row_devs * CAP
    send_target = jnp.where(remote, slot_of, slot_total)
    sending = jax.ops.segment_sum(contrib_flat, send_target, num_segments=slot_total + 1)[
        :slot_total
    ]
    sending = sending.reshape(row_devs, CAP, feat_rows, tile_n)
    arrived = lax.all_to_all(
        sending.astype(jnp.bfloat16), "rows", split_axis=0, concat_axis=0, tiled=True
    ).astype(sending.dtype)
    arrived_flat = arrived.reshape(slot_total, feat_rows * tile_n)
    block_ids = jnp.arange(blocks_n, dtype=jnp.int32)
    slot_block = jnp.sum(selector.astype(jnp.int32) * block_ids[None, None, :], axis=2)
    slot_used = jnp.any(selector, axis=2)
    peer_target = jnp.where(slot_used, slot_block, blocks_n).reshape(-1)
    from_peers = jax.ops.segment_sum(arrived_flat, peer_target, num_segments=blocks_n + 1)[
        :blocks_n
    ]
    self_target = jnp.where(remote, blocks_n, block_pos)
    from_self = jax.ops.segment_sum(contrib_flat, self_target, num_segments=blocks_n + 1)[:blocks_n]
    summed = (from_peers + from_self).reshape(blocks_n, feat_rows, tile_n)
    feat_grad = summed.transpose(1, 0, 2).reshape(feat_rows, node_cols)
    return (output_t, weight_grad, feat_grad)


def solution(mesh):
    return jax.shard_map(
        body,
        mesh=mesh,
        in_specs=(P("cols", "rows"), P(), P("rows", None, None, None), P(), P("cols", "rows")),
        out_specs=(P("cols", "rows"), P("cols", None), P("cols", "rows")),
        check_vma=False,
    )
```

profile of v0, /device:TPU:0, one launch (start us, length us, event | category | flops | bytes accessed | tf_op | source)
XLA Modules:
  0.0 143.8 jit_solution(9876244328487271256)
XLA Ops:
  7.2 0.8 copy.41
  8.0 0.8 fusion.39
  9.8 0.9 copy.60
  10.9 0.7 copy.44
  11.7 7.3 %all-to-all-start = ((bf16[8,4,32,128]{3,2,1,0:T(8,128)(2,1)}), bf16[8,4,32,128]{3,2,1,0:T(8,128)(2,1)S(1)}, u32[]{:S(2)}, u32[]{:S(2)}) async-start(bf16[8,4,32,128]{3,2,1,0:T(8,128)(2,1)} %copy.44), calls=%async_computation | async-start | bytes 524288 | tf_op jit(solution)/shard_map/all_to_all | solution.py:47
  19.4 1.9 %gather_fusion = s32[256]{0:T(256)S(1)} fusion(s32[128]{0:T(128)S(1)} %sub.23, s32[1024]{0:T(1024)S(1)} %pad_clamp_fusion.2), kind=kCustom, calls=%fused_computation | custom fusion | bytes 3072 | tf_op jit(solution)/shard_map/gather | solution.py:39
  21.4 0.9 bitcast_bitcast_fusion
  22.3 1.0 gather_fusion.2
  23.4 4.6 %all-to-all-done = bf16[8,4,32,128]{3,2,1,0:T(8,128)(2,1)S(1)} async-done(((bf16[8,4,32,128]{3,2,1,0:T(8,128)(2,1)}), bf16[8,4,32,128]{3,2,1,0:T(8,128)(2,1)S(1)}, u32[]{:S(2)}, u32[]{:S(2)}) %all-to-all-start) | async-done | bytes 262176 | tf_op jit(solution)/shard_map/all_to_all | solution.py:47
  27.9 2.2 %gather_fusion.1 = bf16[256,32,128]{2,1,0:T(8,128)(2,1)} fusion(bf16[32,32,128]{2,1,0:T(8,128)(2,1)S(1)} %bitcast.83, s32[1024]{0:T(1024)S(1)} %pad_clamp_fusion.1), kind=kCustom, calls=%fused_computation.1 | custom fusion | bytes 4195328 | tf_op jit(solution)/shard_map/gather | solution.py:48
  30.1 6.9 %fusion.16 = bf16[16,4,8,128]{3,2,1,0:T(8,128)(2,1)S(1)} fusion(bf16[16,16,128,128]{3,2,1,0:T(8,128)(2,1)} %param.7, bf16[16,16,32,128]{3,2,1,0:T(8,128)(2,1)} %bitcast.85, bf16[16,16,32,128]{3,2,1,0:T(8,128)(2,1)S(1)} %bitcast.84, pred[16,16]{1,0:T(8,128)(4,1)S(1)} %copy.40), kind=kOutput, calls=%fused_computation.20 | convolution fusion | flops 269549568 | bytes 12714240 | tf_op jit(solution)/shard_map/bkfj,bkij->fbi/dot_general | solution.py:53
  37.1 7.3 %all_gather.6 = bf16[128,2048]{1,0:T(8,128)(2,1)S(1)} all-gather(bf16[32,2048]{1,0:T(8,128)(2,1)S(1)} %bitcast.90), channel_id=1, replica_groups=mesh['rows'=8,'cols'=4] {'cols'}, dimensions={0}, use_global_device_ids=true | all-gather | bytes 655360 | tf_op jit(solution)/shard_map/all_gather | solution.py:58
  44.4 1.3 multiply_convert_fusion
  46.2 14.7 %all-gather.2.cloned.1.call-done = bf16[256,2048]{1,0:T(8,128)(2,1)} async-done(((bf16[64,2048]{1,0:T(8,128)(2,1)}), bf16[256,2048]{1,0:T(8,128)(2,1)}) %all-gather.2.cloned.1.call-update) | async-done | bytes 1048592 | tf_op jit(solution)/shard_map/all_gather | solution.py:68
  60.9 1.5 %fusion.15 = bf16[4,8,16,128]{3,1,2,0:T(8,128)(2,1)S(1)} fusion(bf16[256,2048]{1,0:T(8,128)(2,1)} %all-gather.2.cloned.1.call-done, bf16[128,256]{1,0:T(8,128)(2,1)S(1)} %copy-done, s32[]{:T(128)S(6)} %select_n.136), kind=kOutput, calls=%fused_computation.19 | convolution fusion | flops 33619968 | bytes 1196036 | tf_op jit(solution)/shard_map/dot_general | solution.py:69
  62.5 6.5 %fusion.28 = f32[16,32,16,128]{3,1,2,0:T(8,128)} fusion(bf16[16,16,128,128]{3,2,1,0:T(8,128)(2,1)} %param.7, bf16[32,16,128,1]{2,1,0,3:T(8,128)(2,1)S(1)} %bitcast.88), kind=kOutput, calls=%fused_computation.38 | convolution fusion | flops 268435456 | bytes 12713984 | tf_op jit(solution)/shard_map/fbi,bkij->bkfj/dot_general | solution.py:76
  69.0 10.2 %scatter_custom_fusion.2 = f32[17,4096]{1,0:T(8,128)S(1)} fusion(s32[256]{0:T(256)S(1)} %bitcast.99, f32[32,8,32,128]{3,2,1,0:T(8,128)} %bitcast.81, f32[]{:T(128)} %constant.69.clone.1), kind=kCustom, calls=%fused_computation.6 | custom fusion | flops 1048576 | bytes 4472836 | tf_op jit(solution)/shard_map/scatter-add | solution.py:101
  79.3 10.2 %scatter_custom_fusion = f32[33,4096]{1,0:T(8,128)S(1)} fusion(s32[256]{0:T(256)S(1)} %bitcast.98, f32[32,8,32,128]{3,2,1,0:T(8,128)} %bitcast.82, f32[]{:T(128)} %constant.69.clone.1), kind=kCustom, calls=%fused_computation.8 | custom fusion | flops 1048576 | bytes 4734980 | tf_op jit(solution)/shard_map/scatter-add | solution.py:85
  89.5 0.7 copy.63
  90.3 5.5 %all-to-all-start.1 = ((bf16[8,4,32,128]{3,2,1,0:T(8,128)(2,1)}), bf16[8,4,32,128]{3,2,1,0:T(8,128)(2,1)S(1)}, u32[]{:S(2)}, u32[]{:S(2)}) async-start(bf16[8,4,32,128]{3,2,1,0:T(8,128)(2,1)} %bitcast.37), calls=%async_computation.1 | async-start | bytes 524288 | tf_op jit(solution)/shard_map/all_to_all | solution.py:89
  96.2 37.6 %psum.7 = f32[32,256]{1,0:T(8,128)S(1)} all-reduce(f32[32,256]{1,0:T(8,128)S(1)} %fusion.45), channel_id=1, replica_groups=mesh['rows'=8,'cols'=4] {'rows'}, use_global_device_ids=true, to_apply=%region_4.5 | all-reduce | flops 8192 | bytes 65536 | tf_op jit(solution)/shard_map/psum | solution.py:74
  133.8 0.6 broadcast_multiply_fusion
  134.4 1.7 %scatter_custom_fusion.1 = f32[17,4096]{1,0:T(8,128)S(1)} fusion(s32[32]{0:T(128)S(1)} %reshape.376, f32[4,8,32,128]{3,2,1,0:T(8,128)S(1)} %bitcast_convert_fusion, f32[]{:T(128)} %constant.69.clone.1), kind=kCustom, calls=%fused_computation.21 | custom fusion | flops 131072 | bytes 802820 | tf_op jit(solution)/shard_map/scatter-add | solution.py:97
  136.2 0.7 copy.84
  (44 shorter events, 2.8 us)
Async XLA Ops:
  7.2 37.3 %copy-start = (bf16[128,256]{1,0:T(8,128)(2,1)S(1)}, bf16[128,256]{1,0:T(8,128)(2,1)}, u32[]{:S(2)}) copy-start(bf16[128,256]{1,0:T(8,128)(2,1)} %param.8) | copy-start | bytes 196612
  11.7 16.2 %all-to-all-start = ((bf16[8,4,32,128]{3,2,1,0:T(8,128)(2,1)}), bf16[8,4,32,128]{3,2,1,0:T(8,128)(2,1)S(1)}, u32[]{:S(2)}, u32[]{:S(2)}) async-start(bf16[8,4,32,128]{3,2,1,0:T(8,128)(2,1)} %copy.44), calls=%async_computation | async-start | bytes 524288 | tf_op jit(solution)/shard_map/all_to_all | solution.py:47
  19.0 41.9 %all-gather.2.cloned.1.call-start = ((), (), s32[]{:S(2)}) async-start(), calls=%async_computation.2 | async-start | bytes 1310720 | tf_op jit(solution)/shard_map/all_gather | solution.py:68
  30.1 14.3 %copy-start.2 = (bf16[64,2048]{1,0:T(8,128)(2,1)S(1)}, bf16[64,2048]{1,0:T(8,128)(2,1)}, u32[]{:S(2)}) copy-start(bf16[64,2048]{1,0:T(8,128)(2,1)} %param.9) | copy-start | bytes 786436
  79.3 16.5 %copy-start.1 = (bf16[256,2048]{1,0:T(8,128)(2,1)S(1)}, bf16[256,2048]{1,0:T(8,128)(2,1)}, u32[]{:S(2)}) copy-start(bf16[256,2048]{1,0:T(8,128)(2,1)} %all-gather.2.cloned.1.call-done) | copy-start | bytes 3145732
  90.3 44.1 %all-to-all-start.1 = ((bf16[8,4,32,128]{3,2,1,0:T(8,128)(2,1)}), bf16[8,4,32,128]{3,2,1,0:T(8,128)(2,1)S(1)}, u32[]{:S(2)}, u32[]{:S(2)}) async-start(bf16[8,4,32,128]{3,2,1,0:T(8,128)(2,1)} %bitcast.37), calls=%async_computation.1 | async-start | bytes 524288 | tf_op jit(solution)/shard_map/all_to_all | solution.py:89
Sparse Core Ops, SparseCore 0:
  45.9 15.0 all-gather.1
where the time goes:
time: 144 us
  blocking collectives  44.9 us (31%)
  other arithmetic  24.7 us (17%)
  waiting for transfers between devices  19.3 us (13%)
  matrix products  16.9 us (12%)
  between operations  14.2 us (10%)
  starting transfers between devices  12.9 us (9%)
  local copies, waits for them, and re-layouts  10.8 us (8%)
    psum x1, blocking collectives, body(): weight_grad = lax.psum(block_grad, 'rows') * grad_scale  37.6 us
    all_gather x1, waiting for transfers between devices, body(): portion = lax.all_gather(pre_grad, 'cols', axis=0, tiled=True)  14.7 us
    scatter-add x1, other arithmetic, body(): jax.ops.segment_sum(contrib_flat, self_target, num_segments=blocks_n + 1)  10.2 us
    scatter-add x1, other arithmetic, body(): jax.ops.segment_sum(contrib_flat, send_target, num_segments=slot_total + 1)  10.2 us
    all_gather x1, blocking collectives, body(): lax.all_gather(aggregated, 'cols', axis=0, tiled=True)  7.35 us
    all_to_all x1, starting transfers between devices, body(): lax.all_to_all(outgoing, 'rows', split_axis=0, concat_axis=0, tiled=True)  7.31 us
    dot_general x1, matrix products, body(): jnp.einsum('bkfj,bkij->fbi', picked, adj_weight, preferred_element_type=j...  6.91 us
    dot_general x1, matrix products, body(): jnp.einsum('fbi,bkij->bkfj', agg_grad.reshape(feat_rows, blocks_n, tile_n...  6.54 us
  transfers between devices with their start and end apart: 3, of which 2 were waited for; matrix products, arithmetic and copies ran while one was open for 4% of the time, Pallas kernels for 0%

commit v1 on v0

--- a/solution.py
+++ b/solution.py
@@ -5,6 +5,11 @@
 from jax.sharding import PartitionSpec as P
 
 CAP = 4
+
+
+def _put_core(content):
+    part_next = jnp.sum(lax.all_gather(content, "rows"), 0)
+    return part_next
 
 
 def body(feats_t, adj_index, adj_weight, weight, cotangent_t):
@@ -71,7 +76,7 @@
         aggregated, portion, (((1,), (1,)), ((), ())), preferred_element_type=jnp.float32
     )
     grad_scale = 1.0 / math.sqrt(node_cols * row_devs)
-    weight_grad = lax.psum(block_grad, "rows") * grad_scale
+    weight_grad = _put_core(block_grad) * grad_scale
     agg_grad = grad_acc.astype(jnp.bfloat16)
     contrib = jnp.einsum(
         "fbi,bkij->bkfj",

time: 144 us -> 140 us (0.972)
  blocking collectives: 44.9 us -> 40.6 us
    psum x1 -> x0, blocking collectives: 37.6 us -> none  [body(): weight_grad = lax.psum(block_grad, 'rows') * grad_scale]
    all_gather x0 -> x1, blocking collectives: none -> 33.3 us  [_put_core(): part_next = jnp.sum(lax.all_gather(content, 'rows'), 0)]
  transfers between devices with their start and end apart: 3 -> 3, of which waited for: 2 -> 2; matrix products, arithmetic and copies ran while one was open for 4% -> 11% of each run, Pallas kernels for 0% -> 0%
where the time goes in v1:
time: 140 us; the launch traced here: 139 us
  blocking collectives  40.6 us (29%)
  other arithmetic  24.5 us (18%)
  waiting for transfers between devices  19.3 us (14%)
  matrix products  16.9 us (12%)
  between operations  14.2 us (10%)
  starting transfers between devices  12.9 us (9%)
  local copies, waits for them, and re-layouts  10.8 us (8%)
    all_gather x1, blocking collectives, _put_core(): part_next = jnp.sum(lax.all_gather(content, 'rows'), 0)  33.3 us
    all_gather x1, waiting for transfers between devices, body(): portion = lax.all_gather(pre_grad, 'cols', axis=0, tiled=True)  14.7 us
    scatter-add x1, other arithmetic, body(): jax.ops.segment_sum(contrib_flat, send_target, num_segments=slot_total + 1)  10.2 us
    scatter-add x1, other arithmetic, body(): jax.ops.segment_sum(contrib_flat, self_target, num_segments=blocks_n + 1)  10 us
    all_gather x1, blocking collectives, body(): lax.all_gather(aggregated, 'cols', axis=0, tiled=True)  7.35 us
    all_to_all x1, starting transfers between devices, body(): lax.all_to_all(outgoing, 'rows', split_axis=0, concat_axis=0, tiled=True)  7.31 us
    dot_general x1, matrix products, body(): jnp.einsum('bkfj,bkij->fbi', picked, adj_weight, preferred_element_type=j...  6.91 us
    dot_general x1, matrix products, body(): jnp.einsum('fbi,bkij->bkfj', agg_grad.reshape(feat_rows, blocks_n, tile_n...  6.54 us
  transfers between devices with their start and end apart: 3, of which 2 were waited for; matrix products, arithmetic and copies ran while one was open for 11% of the time, Pallas kernels for 0%

profile of v1, /device:TPU:0, one launch (start us, length us, event | category | flops | bytes accessed | tf_op | source)
XLA Modules:
  0.0 139.3 jit_solution(4189667286631378425)
XLA Ops:
  7.2 0.8 copy.41
  8.0 0.8 fusion.39
  9.8 0.9 copy.60
  10.9 0.7 copy.44
  11.7 7.3 %all-to-all-start = ((bf16[8,4,32,128]{3,2,1,0:T(8,128)(2,1)}), bf16[8,4,32,128]{3,2,1,0:T(8,128)(2,1)S(1)}, u32[]{:S(2)}, u32[]{:S(2)}) async-start(bf16[8,4,32,128]{3,2,1,0:T(8,128)(2,1)} %copy.44), calls=%async_computation | async-start | bytes 524288 | tf_op jit(solution)/shard_map/all_to_all | solution.py:52
  19.4 1.9 %gather_fusion = s32[256]{0:T(256)S(1)} fusion(s32[128]{0:T(128)S(1)} %sub.23, s32[1024]{0:T(1024)S(1)} %pad_clamp_fusion.2), kind=kCustom, calls=%fused_computation | custom fusion | bytes 3072 | tf_op jit(solution)/shard_map/gather | solution.py:44
  21.4 0.9 bitcast_bitcast_fusion
  22.3 1.0 gather_fusion.2
  23.4 4.6 %all-to-all-done = bf16[8,4,32,128]{3,2,1,0:T(8,128)(2,1)S(1)} async-done(((bf16[8,4,32,128]{3,2,1,0:T(8,128)(2,1)}), bf16[8,4,32,128]{3,2,1,0:T(8,128)(2,1)S(1)}, u32[]{:S(2)}, u32[]{:S(2)}) %all-to-all-start) | async-done | bytes 262176 | tf_op jit(solution)/shard_map/all_to_all | solution.py:52
  27.9 2.2 %gather_fusion.1 = bf16[256,32,128]{2,1,0:T(8,128)(2,1)} fusion(bf16[32,32,128]{2,1,0:T(8,128)(2,1)S(1)} %bitcast.84, s32[1024]{0:T(1024)S(1)} %pad_clamp_fusion.1), kind=kCustom, calls=%fused_computation.1 | custom fusion | bytes 4195328 | tf_op jit(solution)/shard_map/gather | solution.py:53
  30.1 6.9 %fusion.16 = bf16[16,4,8,128]{3,2,1,0:T(8,128)(2,1)S(1)} fusion(bf16[16,16,128,128]{3,2,1,0:T(8,128)(2,1)} %param.7, bf16[16,16,32,128]{3,2,1,0:T(8,128)(2,1)} %bitcast.86, bf16[16,16,32,128]{3,2,1,0:T(8,128)(2,1)S(1)} %bitcast.85, pred[16,16]{1,0:T(8,128)(4,1)S(1)} %copy.40), kind=kOutput, calls=%fused_computation.20 | convolution fusion | flops 269549568 | bytes 12714240 | tf_op jit(solution)/shard_map/bkfj,bkij->fbi/dot_general | solution.py:58
  37.1 7.3 %all_gather.12 = bf16[128,2048]{1,0:T(8,128)(2,1)S(1)} all-gather(bf16[32,2048]{1,0:T(8,128)(2,1)S(1)} %bitcast.92), channel_id=1, replica_groups=mesh['rows'=8,'cols'=4] {'cols'}, dimensions={0}, use_global_device_ids=true | all-gather | bytes 655360 | tf_op jit(solution)/shard_map/all_gather | solution.py:63
  44.4 1.3 multiply_convert_fusion
  46.2 14.7 %all-gather.3.cloned.1.call-done = bf16[256,2048]{1,0:T(8,128)(2,1)} async-done(((bf16[64,2048]{1,0:T(8,128)(2,1)}), bf16[256,2048]{1,0:T(8,128)(2,1)}) %all-gather.3.cloned.1.call-update) | async-done | bytes 1048592 | tf_op jit(solution)/shard_map/all_gather | solution.py:73
  60.9 1.5 %fusion.15 = bf16[4,8,16,128]{3,1,2,0:T(8,128)(2,1)S(1)} fusion(bf16[256,2048]{1,0:T(8,128)(2,1)} %all-gather.3.cloned.1.call-done, bf16[128,256]{1,0:T(8,128)(2,1)S(1)} %copy-done, s32[]{:T(128)S(6)} %select_n.136), kind=kOutput, calls=%fused_computation.19 | convolution fusion | flops 33619968 | bytes 1196036 | tf_op jit(solution)/shard_map/dot_general | solution.py:74
  62.5 6.5 %fusion.28 = f32[16,32,16,128]{3,1,2,0:T(8,128)} fusion(bf16[16,16,128,128]{3,2,1,0:T(8,128)(2,1)} %param.7, bf16[32,16,128,1]{2,1,0,3:T(8,128)(2,1)S(1)} %bitcast.90), kind=kOutput, calls=%fused_computation.38 | convolution fusion | flops 268435456 | bytes 12713984 | tf_op jit(solution)/shard_map/fbi,bkij->bkfj/dot_general | solution.py:81
  69.0 10.2 %scatter_custom_fusion = f32[33,4096]{1,0:T(8,128)S(1)} fusion(s32[256]{0:T(256)S(1)} %bitcast.101, f32[32,8,32,128]{3,2,1,0:T(8,128)} %bitcast.82, f32[]{:T(128)} %constant.69.clone.1), kind=kCustom, calls=%fused_computation.8 | custom fusion | flops 1048576 | bytes 4734980 | tf_op jit(solution)/shard_map/scatter-add | solution.py:90
  79.2 0.7 copy.63
  80.0 5.5 %all-to-all-start.1 = ((bf16[8,4,32,128]{3,2,1,0:T(8,128)(2,1)}), bf16[8,4,32,128]{3,2,1,0:T(8,128)(2,1)S(1)}, u32[]{:S(2)}, u32[]{:S(2)}) async-start(bf16[8,4,32,128]{3,2,1,0:T(8,128)(2,1)} %bitcast.38), calls=%async_computation.1 | async-start | bytes 524288 | tf_op jit(solution)/shard_map/all_to_all | solution.py:94
  85.9 33.3 %all-gather = f32[256,256]{1,0:T(8,128)S(1)} all-gather(f32[32,256]{1,0:T(8,128)S(1)} %fusion.45), channel_id=2, replica_groups=mesh['rows'=8,'cols'=4] {'rows'}, dimensions={0}, use_global_device_ids=true | all-gather | bytes 294912 | tf_op jit(solution)/shard_map/all_gather | solution.py:11
  119.2 10.0 %scatter_custom_fusion.2 = f32[17,4096]{1,0:T(8,128)S(1)} fusion(s32[256]{0:T(256)S(1)} %bitcast.100, f32[32,8,32,128]{3,2,1,0:T(8,128)} %bitcast.83, f32[]{:T(128)} %constant.69.clone.1), kind=kCustom, calls=%fused_computation.6 | custom fusion | flops 1048576 | bytes 4472836 | tf_op jit(solution)/shard_map/scatter-add | solution.py:106
  129.2 0.6 broadcast_multiply_fusion
  129.9 1.7 %scatter_custom_fusion.1 = f32[17,4096]{1,0:T(8,128)S(1)} fusion(s32[32]{0:T(128)S(1)} %reshape.376, f32[4,8,32,128]{3,2,1,0:T(8,128)S(1)} %bitcast_convert_fusion, f32[]{:T(128)} %constant.69.clone.1), kind=kCustom, calls=%fused_computation.21 | custom fusion | flops 131072 | bytes 802820 | tf_op jit(solution)/shard_map/scatter-add | solution.py:102
  131.7 0.7 copy.84
  (45 shorter events, 2.9 us)
Async XLA Ops:
  7.2 37.3 %copy-start = (bf16[128,256]{1,0:T(8,128)(2,1)S(1)}, bf16[128,256]{1,0:T(8,128)(2,1)}, u32[]{:S(2)}) copy-start(bf16[128,256]{1,0:T(8,128)(2,1)} %param.8) | copy-start | bytes 196612
  11.7 16.2 %all-to-all-start = ((bf16[8,4,32,128]{3,2,1,0:T(8,128)(2,1)}), bf16[8,4,32,128]{3,2,1,0:T(8,128)(2,1)S(1)}, u32[]{:S(2)}, u32[]{:S(2)}) async-start(bf16[8,4,32,128]{3,2,1,0:T(8,128)(2,1)} %copy.44), calls=%async_computation | async-start | bytes 524288 | tf_op jit(solution)/shard_map/all_to_all | solution.py:52
  19.0 41.9 %all-gather.3.cloned.1.call-start = ((), (), s32[]{:S(2)}) async-start(), calls=%async_computation.2 | async-start | bytes 1310720 | tf_op jit(solution)/shard_map/all_gather | solution.py:73
  30.1 14.3 %copy-start.2 = (bf16[64,2048]{1,0:T(8,128)(2,1)S(1)}, bf16[64,2048]{1,0:T(8,128)(2,1)}, u32[]{:S(2)}) copy-start(bf16[64,2048]{1,0:T(8,128)(2,1)} %param.9) | copy-start | bytes 786436
  69.0 16.5 %copy-start.1 = (bf16[256,2048]{1,0:T(8,128)(2,1)S(1)}, bf16[256,2048]{1,0:T(8,128)(2,1)}, u32[]{:S(2)}) copy-start(bf16[256,2048]{1,0:T(8,128)(2,1)} %all-gather.3.cloned.1.call-done) | copy-start | bytes 3145732
  80.0 49.9 %all-to-all-start.1 = ((bf16[8,4,32,128]{3,2,1,0:T(8,128)(2,1)}), bf16[8,4,32,128]{3,2,1,0:T(8,128)(2,1)S(1)}, u32[]{:S(2)}, u32[]{:S(2)}) async-start(bf16[8,4,32,128]{3,2,1,0:T(8,128)(2,1)} %bitcast.38), calls=%async_computation.1 | async-start | bytes 524288 | tf_op jit(solution)/shard_map/all_to_all | solution.py:94
Sparse Core Ops, SparseCore 0:
  45.9 15.0 all-gather.2
